TPU v7x, 128 devices: a whole 4x4x4 slice. The times are simulated.
128 devices in a mesh: req: 4 (over y), seq: 32 (over x, z, core).
Axes of the slice: x: 4, y: 4, z: 4, core: 2. Of those that a mesh axis runs over, the one named last changes fastest.
Arguments:
- inputs: bfloat16 [1, 32, 5120], P(None, 'req', 'seq'), may hold values from -6 to 6
- lengths: int32 [32], P('req'), may hold values from 4 to 4096, as said below
- targets: int32 [1, 32], replicated, may hold values from 0 to 81919
- cache_keys: bfloat16 [32, 4096, 8, 128], P('req', 'seq'), may hold values from -192 to 192
- cache_values: bfloat16 [32, 4096, 8, 128], P('req', 'seq'), may hold values from -30 to 30
- attention_gain: float32 [5120], replicated, may hold values from 0.1 to 1.9
- packed_weight: bfloat16 [5120, 7168], P(None, 'seq'), may hold values from -0.078125 to 0.078125
- packed_bias: float32 [7168], P('seq'), may hold values from -3 to 3
- out_weight: bfloat16 [5120, 5120], P(None, 'seq'), may hold values from -0.078125 to 0.078125
- feedforward_gain: float32 [5120], replicated, may hold values from 0.1 to 1.9
- gate_weight: bfloat16 [5120, 27648], P(None, ('req', 'seq')), may hold values from -0.078125 to 0.078125
- up_weight: bfloat16 [5120, 27648], P(None, ('req', 'seq')), may hold values from -0.078125 to 0.078125
- down_weight: bfloat16 [27648, 5120], P(('req', 'seq')), may hold values from -0.125 to 0.125
- final_gain: float32 [5120], replicated, may hold values from 0.1 to 1.9
- head_weight: bfloat16 [5120, 81920], P(None, ('req', 'seq')), may hold values from -7.5467294 to 7.5467294
Outputs:
- hidden_states: bfloat16 [1, 32, 5120], P(None, 'req', 'seq')
- log_probs: float32 [1, 32], replicated
Inputs may be any that keep to these rules, and one draw needn't show every extreme that they name: Every draw has a request with exactly 4096 cached positions; lengths are spread evenly in the logarithm.
All inputs are finite; a program needn't handle non-finite values.
Results may differ from a plain program's by a relative error of at most 0.013.
Values may be sent and summed in bfloat16 or wider, within the bound.
A program may use at most 128 MiB of HBM per device.

v0:
```python
import jax
import jax.numpy as jnp
from jax import lax
from jax.sharding import PartitionSpec as P

EPSILON = 1e-06
THETA = 1000000.0
NEGATIVE = -1e30


def merged_2(part, axis, combine):
    gathered = jax.tree.map(lambda a: lax.all_gather(a, axis), part)

    def take(source):
        return jax.tree.map(lambda a: lax.dynamic_index_in_dim(a, source, 0, False), gathered)

    return lax.fori_loop(
        1, lax.axis_size(axis), lambda source, state: combine(state, take(source)), take(0)
    )


def normalize(values, gain_vector):
    wide = values.astype(jnp.float32)
    return wide * lax.rsqrt(jnp.mean(wide * wide, axis=-1, keepdims=True) + EPSILON) * gain_vector


def rotate(vectors, position):
    half_dim = vectors.shape[-1] // 2
    inverse = THETA ** (-(jnp.arange(half_dim, dtype=jnp.float32) * 2.0 / vectors.shape[-1]))
    angle = position[..., None] * inverse
    cosine = jnp.cos(angle)
    sine = jnp.sin(angle)
    first_half = vectors[..., :half_dim]
    second_half = vectors[..., half_dim:]
    return jnp.concatenate(
        [first_half * cosine - second_half * sine, second_half * cosine + first_half * sine],
        axis=-1,
    )


def local_attention(grouped, key_block, value_block, live_mask):
    scale_factor = grouped.shape[-1] ** (-0.5)
    scores = (
        jnp.einsum("gkjd,gpkd->gkjp", grouped, key_block, preferred_element_type=jnp.float32)
        * scale_factor
    )
    visible = live_mask[:, None, None, :]
    scores = jnp.where(visible, scores, NEGATIVE)
    top_score = scores.max(axis=-1)
    weights = jnp.where(visible, jnp.exp(scores - top_score[..., None]), 0.0).astype(jnp.bfloat16)
    total = weights.astype(jnp.float32).sum(axis=-1)
    summed = jnp.einsum("gkjp,gpkd->gkjd", weights, value_block, preferred_element_type=jnp.float32)
    return (top_score, total, summed)


def join_parts(earlier, later):
    top_score = jnp.maximum(earlier[0], later[0])
    factor_one = jnp.exp(earlier[0] - top_score)
    factor_two = jnp.exp(later[0] - top_score)
    total = earlier[1] * factor_one + later[1] * factor_two
    summed = earlier[2] * factor_one[..., None] + later[2] * factor_two[..., None]
    return (top_score, total, summed)


def full_features(block):
    return lax.all_gather(block, "seq", axis=1, tiled=True)


def all_requests(row_block):
    return lax.all_gather(row_block, "req", axis=0, tiled=True)


def per_device(
    inputs,
    lengths,
    targets,
    cache_keys,
    cache_values,
    attention_gain,
    packed_weight,
    packed_bias,
    out_weight,
    feedforward_gain,
    gate_weight,
    up_weight,
    down_weight,
    final_gain,
    head_weight,
):
    step_count, group_rows, feature_part = inputs.shape
    positions = cache_keys.shape[1]
    kv_heads = cache_keys.shape[2]
    head_size = cache_keys.shape[3]
    model_width = attention_gain.shape[0]
    query_heads = model_width // head_size
    per_group = query_heads // kv_heads
    query_width = query_heads * head_size
    key_width = kv_heads * head_size
    req_count = lax.axis_size("req")
    seq_count = lax.axis_size("seq")
    seq_position = lax.axis_index("seq")
    cache_start = seq_position * positions
    cached_live = (cache_start + jnp.arange(positions, dtype=jnp.int32))[None, :] < lengths[:, None]
    leading = seq_position == 0
    vocab_part = head_weight.shape[1]
    vocab_start = (lax.axis_index("req") * seq_count + seq_position) * vocab_part
    vocab_ids = vocab_start + jnp.arange(vocab_part, dtype=jnp.int32)
    current = inputs[0]
    row_block = full_features(current)
    normed = normalize(row_block, attention_gain).astype(jnp.bfloat16)
    packed_part = (
        jnp.dot(normed, packed_weight, preferred_element_type=jnp.float32) + packed_bias
    ).astype(jnp.bfloat16)
    packed = lax.all_gather(packed_part, "seq", axis=1, tiled=True)
    position = (lengths + 0).astype(jnp.float32)[:, None]
    query = rotate(
        packed[:, :query_width].astype(jnp.float32).reshape(group_rows, query_heads, head_size),
        position,
    ).astype(jnp.bfloat16)
    grouped = query.reshape(group_rows, kv_heads, per_group, head_size)
    key_now = rotate(
        packed[:, query_width : query_width + key_width]
        .astype(jnp.float32)
        .reshape(group_rows, kv_heads, head_size),
        position,
    ).astype(jnp.bfloat16)
    new_keys = [key_now]
    new_values = [packed[:, query_width + key_width :].reshape(group_rows, kv_heads, head_size)]
    cached_parts = local_attention(grouped, cache_keys, cache_values, cached_live)
    recent_keys = jnp.stack(new_keys, axis=1)
    recent_values = jnp.stack(new_values, axis=1)
    recent_live = jnp.broadcast_to(leading, (group_rows, 1))
    recent_parts = local_attention(grouped, recent_keys, recent_values, recent_live)
    local_parts = join_parts(cached_parts, recent_parts)
    merged = merged_2(local_parts, "seq", join_parts)
    merged_total = merged[1]
    merged_sum = merged[2]
    attention = (
        (merged_sum / merged_total[..., None]).reshape(group_rows, query_width).astype(jnp.bfloat16)
    )
    mixed = (
        current.astype(jnp.float32)
        + jnp.dot(attention, out_weight, preferred_element_type=jnp.float32)
    ).astype(jnp.bfloat16)
    everyone = all_requests(full_features(mixed))
    normed = normalize(everyone, feedforward_gain).astype(jnp.bfloat16)
    gate_part = jnp.dot(normed, gate_weight, preferred_element_type=jnp.float32)
    up_part = jnp.dot(normed, up_weight, preferred_element_type=jnp.float32)
    hidden = (jax.nn.silu(gate_part) * up_part).astype(jnp.bfloat16)
    partial_out = jnp.dot(hidden, down_weight, preferred_element_type=jnp.float32)
    arranged = (
        partial_out.reshape(req_count, group_rows, seq_count, feature_part)
        .transpose(0, 2, 1, 3)
        .reshape(req_count * seq_count * group_rows, feature_part)
    )
    feedforward_out = lax.psum_scatter(arranged, ("req", "seq"), scatter_dimension=0, tiled=True)
    result = (mixed.astype(jnp.float32) + feedforward_out).astype(jnp.bfloat16)
    states = [result]
    final_rows = all_requests(full_features(result))
    normed = normalize(final_rows, final_gain).astype(jnp.bfloat16)
    logits = jnp.dot(normed, head_weight, preferred_element_type=jnp.float32)
    matches = vocab_ids[None, :] == targets[0][:, None]
    picked = jnp.sum(jnp.where(matches, logits, 0.0), axis=-1)
    global_top = lax.pmax(logits.max(axis=-1), ("req", "seq"))
    global_total, global_pick = lax.psum(
        (jnp.sum(jnp.exp(logits - global_top[:, None]), axis=-1), picked), ("req", "seq")
    )
    probabilities = [global_pick - (global_top + jnp.log(global_total))]
    return (jnp.stack(states), jnp.stack(probabilities))


def solution(mesh):
    return jax.shard_map(
        per_device,
        mesh=mesh,
        in_specs=(
            P(None, "req", "seq"),
            P("req"),
            P(),
            P("req", "seq", None, None),
            P("req", "seq", None, None),
            P(),
            P(None, "seq"),
            P("seq"),
            P(None, "seq"),
            P(),
            P(None, ("req", "seq")),
            P(None, ("req", "seq")),
            P(("req", "seq"), None),
            P(),
            P(None, ("req", "seq")),
        ),
        out_specs=(P(None, "req", "seq"), P()),
        check_vma=False,
    )
```

profile of v0, /device:TPU:1, one launch (start us, length us, event | category | flops | bytes accessed | tf_op | source)
XLA Modules:
  0.0 1061.8 jit_solution(9395572796793593386)
XLA Ops:
  7.2 1.0 copy.71
  8.2 29.3 %all-gather = bf16[1,8,5120]{1,0,2:T(2,128)(2,1)S(1)} all-gather(bf16[1,8,160]{1,0,2:T(2,128)(2,1)S(1)} %copy.71), channel_id=2, replica_groups=mesh['req'=4,'seq'=32] {'seq'}, dimensions={2}, use_global_device_ids=true | all-gather | bytes 84480 | tf_op jit(solution)/shard_map/all_gather | solution.py:66
  37.5 2.8 convert_element_type.86
  41.0 1.7 fusion.28
  42.7 24.1 %all-gather.4 = bf16[32,224,8]{1,2,0:T(8,128)(2,1)S(1)} all-gather(bf16[1,224,8]{1,2,0:T(8,128)(2,1)S(1)} %fusion.28), channel_id=1, replica_groups=mesh['req'=4,'seq'=32] {'seq'}, dimensions={0}, use_global_device_ids=true | all-gather | bytes 118272 | tf_op jit(solution)/shard_map/all_gather | solution.py:114
  67.9 3.1 fusion.65
  73.0 22.7 %all-gather.1 = f32[256,8,5]{1,0,2:T(8,128)S(1)} all-gather(f32[8,8,5]{1,0,2:T(8,128)S(1)} %copy.76), channel_id=3, replica_groups=mesh['req'=4,'seq'=32] {'seq'}, dimensions={0}, use_global_device_ids=true | all-gather | bytes 42240 | tf_op jit(solution)/shard_map/all_gather | solution.py:12
  95.8 26.8 %all-gather.2 = f32[256,8,5]{1,0,2:T(8,128)S(1)} all-gather(f32[8,8,5]{1,0,2:T(8,128)S(1)} %copy.77), channel_id=4, replica_groups=mesh['req'=4,'seq'=32] {'seq'}, dimensions={0}, use_global_device_ids=true | all-gather | bytes 42240 | tf_op jit(solution)/shard_map/all_gather | solution.py:12
  124.5 68.8 %while.19 = (s32[]{:T(128)}, f32[8,8,5]{1,0,2:T(8,128)S(1)}, f32[8,8,5]{1,0,2:T(8,128)S(1)}, f32[8,8,5,128]{3,2,1,0:T(8,128)S(1)}, f32[32,8,8,5]{2,1,0,3:T(8,128...) while((s32[]{:T(128)}, f32[8,8,5]{1,0,2:T(8,128)S(1)}, ...), condition=%wide.region_4.5_spmd, body=%wide.region_3.4_spmd.sunk | while | flops 124805 | bytes 837271 | solution.py:17
  125.2 0.9 constant_dynamic-slice_fusion.2
  127.5 0.9 constant_dynamic-slice_fusion.2
  129.7 0.9 constant_dynamic-slice_fusion.2
  131.9 0.9 constant_dynamic-slice_fusion.2
  134.1 0.9 constant_dynamic-slice_fusion.2
  136.4 0.9 constant_dynamic-slice_fusion.2
  138.6 0.9 constant_dynamic-slice_fusion.2
  140.8 0.9 constant_dynamic-slice_fusion.2
  143.0 0.9 constant_dynamic-slice_fusion.2
  193.7 2.0 fusion.27
  195.7 22.5 %all-gather.5 = bf16[32,160,8]{1,2,0:T(8,128)(2,1)S(1)} all-gather(bf16[1,160,8]{1,2,0:T(8,128)(2,1)S(1)} %bitcast.100), channel_id=1, replica_groups=mesh['req'=4,'seq'=32] {'seq'}, dimensions={0}, use_global_device_ids=true | all-gather | bytes 84480 | tf_op jit(solution)/shard_map/all_gather | solution.py:66
  218.4 10.4 all_gather.39
  229.0 2.4 fusion.41
  231.4 4.8 fusion.24
  236.2 1.7 reshape.215
  237.9 1.6 copy.89
  239.5 640.4 %reduce-scatter.2.cloned.1.call-done = f32[8,160]{1,0:T(8,128)} async-done(((f32[1024,160]{1,0:T(8,128)}), f32[8,160]{1,0:T(8,128)}) %reduce-scatter.2.cloned.1.call-update) | async-done | bytes 5136 | tf_op jit(solution)/shard_map/reduce_scatter | solution.py:156
  879.9 1.3 fusion.60
  881.2 28.5 %all-gather.6 = bf16[32,160,8]{1,2,0:T(8,128)(2,1)S(1)} all-gather(bf16[1,160,8]{1,2,0:T(8,128)(2,1)S(1)} %get-tuple-element.235), channel_id=1, replica_groups=mesh['req'=4,'seq'=32] {'seq'}, dimensions={0}, use_global_device_ids=true | all-gather | bytes 84480 | tf_op jit(solution)/shard_map/all_gather | solution.py:66
  909.9 9.5 all_gather.41
  919.6 4.2 fusion.66
  923.8 66.0 %pmax.7 = f32[32]{0:T(128)S(1)} all-reduce(f32[32]{0:T(128)S(1)} %get-tuple-element.241), channel_id=1, replica_groups=mesh['req'=4,'seq'=32] {'req','seq'}, use_global_device_ids=true, to_apply=%region_11.12 | all-reduce | flops 32 | bytes 256 | tf_op jit(solution)/shard_map/pmax | solution.py:164
  990.0 64.4 %all-reduce = (f32[32]{0:T(128)S(1)}, f32[32]{0:T(128)S(1)}) all-reduce(f32[32]{0:T(128)S(1)} %get-tuple-element.203, f32[32]{0:T(128)S(1)} %get-tuple-element.202), channel_id=1, replica_groups=mesh['req'=4,'seq'=32] {'req','seq'}, use_global_device_ids=true, to_apply=%region_9.10 | all-reduce | flops 64 | bytes 512 | tf_op jit(solution)/shard_map/psum | solution.py:165
  (213 shorter events, 67.2 us)
Async XLA Ops:
  7.2 33.8 %copy-start = (bf16[5120,224]{0,1:T(8,128)(2,1)S(1)}, bf16[5120,224]{0,1:T(8,128)(2,1)}, u32[]{:S(2)}) copy-start(bf16[5120,224]{0,1:T(8,128)(2,1)} %param.23) | copy-start | bytes 6881284
  7.2 116.3 %all-gather.9.cloned.1.call-start = ((), (), s32[]{:S(2)}) async-start(), calls=%async_computation.2 | async-start | bytes 5406720 | tf_op jit(solution)/shard_map/all_gather | solution.py:12
  40.3 0.7 copy-start.4
  40.3 0.7 copy-start.6
  41.0 26.0 %copy-start.8 = (s32[8]{0:T(128)S(1)}, s32[8]{0:T(128)}, u32[]{:S(2)}) copy-start(s32[8]{0:T(128)} %param.18) | copy-start | bytes 100
  67.5 3.8 copy-start.9
  72.8 807.1 %reduce-scatter.2.cloned.1.call-start = ((), (), s32[]{:S(2)}) async-start(), calls=%async_computation.1 | async-start | bytes 1056768 | tf_op jit(solution)/shard_map/reduce_scatter | solution.py:156
  122.6 0.9 copy-start.1
  124.5 69.3 %copy-start.5 = (bf16[1,8,160]{2,1,0:T(8,128)(2,1)S(1)}, bf16[1,8,160]{2,1,0:T(8,128)(2,1)}, u32[]{:S(2)}) copy-start(bf16[1,8,160]{2,1,0:T(8,128)(2,1)} %param.17) | copy-start | bytes 7684
  193.3 35.6 %copy-start.2 = (f32[5120]{0:T(1024)S(1)}, f32[5120]{0:T(1024)}, u32[]{:S(2)}) copy-start(f32[5120]{0:T(1024)} %param.26) | copy-start | bytes 61444
  237.9 681.7 %copy-start.3 = (f32[5120]{0:T(1024)S(1)}, f32[5120]{0:T(1024)}, u32[]{:S(2)}) copy-start(f32[5120]{0:T(1024)} %param.30) | copy-start | bytes 61444
  919.6 70.3 %copy-start.7 = (s32[1,32]{1,0:T(1,128)S(1)}, s32[1,32]{1,0:T(1,128)}, u32[]{:S(2)}) copy-start(s32[1,32]{1,0:T(1,128)} %param.19) | copy-start | bytes 388
Sparse Core Ops, SparseCore 0:
  72.9 47.4 all-gather.8
  239.6 640.2 reduce-scatter.1
where the time goes:
time: 1060 us
  waiting for transfers between devices  640 us (60%)
  blocking collectives  304 us (29%)
  local copies, waits for them, and re-layouts  44.6 us (4%)
  other arithmetic  38.1 us (4%)
  matrix products  19.2 us (2%)
  between operations  14.4 us (1%)
    reduce_scatter x1, waiting for transfers between devices, per_device(): lax.psum_scatter(arranged, ('req', 'seq'), scatter_dimension=0, tiled=True)  640 us
    all_gather x3, blocking collectives, full_features(): return lax.all_gather(block, 'seq', axis=1, tiled=True)  80.2 us
    pmax x1, blocking collectives, per_device(): global_top = lax.pmax(logits.max(axis=-1), ('req', 'seq'))  66 us
    psum x1, blocking collectives, per_device(): lax.psum((jnp.sum(jnp.exp(logits - global_top[:, None]), axis=-1), picked...  64.4 us
    all_gather x2, blocking collectives, merged_2(): gathered = jax.tree.map(lambda a: lax.all_gather(a, axis), part)  49.5 us
    dynamic_slice x34, local copies, waits for them, and re-layouts, take(): lax.dynamic_index_in_dim(a, source, 0, False)  29.9 us
    all_gather x1, blocking collectives, per_device(): packed = lax.all_gather(packed_part, 'seq', axis=1, tiled=True)  24.1 us
    add x32, other arithmetic, join_parts(): total = earlier[1] * factor_one + later[1] * factor_two  23.6 us
  transfers between devices with their start and end apart: 2, of which 1 were waited for; matrix products, arithmetic and copies ran while one was open for 0% of the time, Pallas kernels for 0%

commit v1 on v0

v1 whole, which is shorter than its diff:
```python
import functools

import jax
import jax.numpy as jnp
from jax import lax
from jax.experimental import pallas as pl
from jax.experimental.pallas import tpu as pltpu
from jax.sharding import PartitionSpec as P

EPSILON = 1e-06
THETA = 1000000.0
NEGATIVE = -1e30
MESH = pl.DeviceIdType.MESH
F32 = jnp.float32
BF16 = jnp.bfloat16

REQS = 4
SEQS = 32
ROWS = 8
ALL_ROWS = REQS * ROWS
HEADS = 40
KV = 8
GROUP = HEADS // KV
HEAD = 128
WIDTH = 5120
PART = WIDTH // SEQS
PACKED = 7168
PACKED_PART = PACKED // SEQS
FF_PART = 216
VOCAB_PART = 640
POSITIONS = 128
OWNERS = 20
SLAB = ROWS * HEADS // OWNERS
COLUMNS = WIDTH // OWNERS
SCALE = HEAD**-0.5


def owner_seq(index):
    late = index // 16
    return (1 - late) * 2 * index + late * (10 * (index - 16) + 1)


def matmul_nt(left, right):
    return lax.dot_general(left, right, (((1,), (1,)), ((), ())), preferred_element_type=F32)


def normalized(wide, gain):
    mean = jnp.mean(wide * wide, axis=-1, keepdims=True)
    return (wide * lax.rsqrt(mean + EPSILON) * gain).astype(BF16)


def kernel(
    lengths, targets, x_hbm, keys_hbm, values_hbm, gain1_hbm, packed_hbm, bias_hbm, out_hbm, gain2_hbm,
    gate_hbm, up_hbm, down_hbm, gain3_hbm, head_hbm,
    states_ref, probs_ref,
    keys, values, gain1, packed_w, bias, out_w, gain2, gate_w, up_w, down_w, gain3, head_w,
    xg, big, normed, pk, pkf, qs, kx, vx, of, sf, obuf, orecv, lse_s, ag, af, mg, fs, frecv, yex, rg, st, sh,
    load_sem, send_sem, recv_sem,
):
    me_req = lax.axis_index("req")
    me = lax.axis_index("seq")
    core = lax.rem(me, 2)
    chip = me // 2
    is_owner = (core == 0) | (lax.rem(chip, 5) == 0)
    mine = (1 - core) * chip + core * (16 + chip // 5)

    loads = []
    for index, (src, dst) in enumerate(
        [
            (x_hbm.at[0], xg.at[me]),
            (gain1_hbm, gain1),
            (bias_hbm, bias),
            (packed_hbm, packed_w),
            (keys_hbm, keys),
            (values_hbm, values),
            (out_hbm, out_w),
            (gain2_hbm, gain2),
            (gate_hbm, gate_w),
            (up_hbm, up_w),
            (down_hbm, down_w),
            (gain3_hbm, gain3),
            (head_hbm, head_w),
        ]
    ):
        copy = pltpu.make_async_copy(src, dst, load_sem.at[index])
        copy.start()
        loads.append(copy)

    barrier = pltpu.get_barrier_semaphore()

    def greet(step, carry):
        peer = lax.rem(me + step, SEQS)
        pl.semaphore_signal(barrier, inc=1, device_id={"seq": peer}, device_id_type=MESH)
        return carry

    lax.fori_loop(1, SEQS, greet, 0)
    for step in range(1, REQS):
        peer = lax.rem(me_req + step, REQS)
        pl.semaphore_signal(barrier, inc=1, device_id={"req": peer}, device_id_type=MESH)
    pl.semaphore_wait(barrier, SEQS - 1 + REQS - 1)

    def remote(src, dst, phase, where):
        return pltpu.make_async_remote_copy(
            src_ref=src,
            dst_ref=dst,
            send_sem=send_sem.at[phase],
            recv_sem=recv_sem.at[phase],
            device_id=where,
            device_id_type=MESH,
        )

    def to_seq(src, dst, phase):
        def body(step, carry):
            remote(src, dst, phase, {"seq": lax.rem(me + step, SEQS)}).start()
            return carry

        lax.fori_loop(1, SEQS, body, 0)

    def to_req(src, dst, phase):
        for step in range(1, REQS):
            remote(src, dst, phase, {"req": lax.rem(me_req + step, REQS)}).start()

    def to_owners(src_of, dst, phase, own_sem):
        def body(step, carry):
            index = lax.rem(me + step, OWNERS)
            peer = owner_seq(index)

            @pl.when(peer != me)
            def _():
                remote(src_of(index), dst, phase, {"seq": peer}).start()

            @pl.when(peer == me)
            def _():
                pltpu.make_async_copy(src_of(index), dst, own_sem).start()

            return carry

        lax.fori_loop(0, OWNERS, body, 0)

    def drain(ref, sem):
        pltpu.make_async_copy(ref, ref, sem).wait()

    to_seq(x_hbm.at[0], xg.at[me], 0)

    inverse = jnp.exp(
        lax.rem(lax.broadcasted_iota(jnp.int32, (ROWS, HEAD), 1), HEAD // 2).astype(F32)
        * (-2.0 / HEAD * 13.815510557964274)
    )
    row_ids = lax.broadcasted_iota(jnp.int32, (ROWS, HEAD), 0)
    position = jnp.zeros((ROWS, HEAD), jnp.int32)
    for row in range(ROWS):
        position = jnp.where(row_ids == row, lengths[row], position)
    angle = position.astype(F32) * inverse
    lane = lax.broadcasted_iota(jnp.int32, (ROWS, HEAD), 1)
    cosine = jnp.cos(angle)
    sine = jnp.sin(angle)
    signed_sine = jnp.where(lane < HEAD // 2, -sine, sine)

    loads[0].wait()
    drain(xg.at[pl.ds(0, SEQS - 1)], recv_sem.at[0])
    for part in range(SEQS):
        big[0:ROWS, PART * part : PART * (part + 1)] = xg[part].astype(F32)
    loads[1].wait()
    normed[0:ROWS, :] = normalized(big[0:ROWS, :], gain1[...])
    loads[2].wait()
    loads[3].wait()
    pk[me] = (matmul_nt(normed[0:ROWS, :], packed_w[...]) + bias[...]).astype(BF16)

    to_seq(pk.at[me], pk.at[me], 1)
    drain(pk.at[pl.ds(0, SEQS - 1)], recv_sem.at[1])
    for part in range(SEQS):
        pkf[:, PACKED_PART * part : PACKED_PART * (part + 1)] = pk[part].astype(F32)

    def rotated(column):
        head = pkf[:, HEAD * column : HEAD * (column + 1)]
        turned = head * cosine + pltpu.roll(head, HEAD // 2, 1) * signed_sine
        return turned.astype(BF16).astype(F32)

    for head in range(HEADS):
        qs[pl.ds(head, ROWS, stride=HEADS), :] = rotated(head)

    loads[4].wait()
    loads[5].wait()
    column = lax.broadcasted_iota(jnp.int32, (HEADS, POSITIONS * KV), 1)
    line = lax.broadcasted_iota(jnp.int32, (HEADS, POSITIONS * KV), 0)
    same = lax.rem(column, KV) == line // GROUP
    spot = me * POSITIONS + column // KV
    place = jnp.where(same, spot, jnp.int32(1 << 30))
    for row in range(ROWS):
        query = qs[HEADS * row : HEADS * (row + 1), :].astype(BF16)
        scores = matmul_nt(query, keys[row]) * SCALE
        live = place < lengths[row]
        scores = jnp.where(live, scores, NEGATIVE)
        top = jnp.max(scores, axis=-1, keepdims=True)
        weights = jnp.where(live, jnp.exp(scores - top), 0.0).astype(BF16)
        total = jnp.sum(weights.astype(F32), axis=-1, keepdims=True)
        summed = jnp.dot(weights, values[row], preferred_element_type=F32)
        some = total > 0.0
        of[HEADS * row : HEADS * (row + 1), :] = summed / jnp.where(some, total, 1.0)
        lse = jnp.where(some, top + jnp.log(jnp.where(some, total, 1.0)), NEGATIVE)
        sf[HEADS * row : HEADS * (row + 1), :] = jnp.broadcast_to(lse, (HEADS, HEAD))

    slab_lane = lax.broadcasted_iota(jnp.int32, (SLAB, HEAD), 1)
    for index in range(OWNERS):
        obuf[index, :, 0:HEAD] = of[SLAB * index : SLAB * (index + 1), :].astype(BF16)
        lse = sf[SLAB * index : SLAB * (index + 1), :]
        high = lse.astype(BF16).astype(F32)
        middle = (lse - high).astype(BF16).astype(F32)
        low = lse - high - middle
        packed_lse = jnp.where(
            slab_lane == 0, high, jnp.where(slab_lane == 1, middle, jnp.where(slab_lane == 2, low, 0.0))
        )
        obuf[index, :, HEAD : 2 * HEAD] = packed_lse.astype(BF16)

    to_owners(lambda index: obuf.at[index], orecv.at[me], 2, load_sem.at[13])

    for head in range(KV):
        new_key = rotated(HEADS + head)
        new_value = pkf[:, HEAD * (HEADS + KV + head) : HEAD * (HEADS + KV + head + 1)]
        for inner in range(GROUP):
            kx[pl.ds(GROUP * head + inner, ROWS, stride=HEADS), :] = new_key
            vx[pl.ds(GROUP * head + inner, ROWS, stride=HEADS), :] = new_value

    @pl.when(is_owner)
    def _():
        lines = pl.ds(pl.multiple_of(mine * SLAB, SLAB), SLAB)
        fresh = jnp.sum(qs[lines, :] * kx[lines, :], axis=-1, keepdims=True) * SCALE
        pltpu.make_async_copy(obuf.at[mine], orecv.at[me], load_sem.at[13]).wait()
        drain(orecv.at[pl.ds(0, SEQS - 1)], recv_sem.at[2])
        top = jnp.broadcast_to(fresh, (SLAB, HEAD))
        for part in range(SEQS):
            lse = jnp.sum(orecv[part, :, HEAD : 2 * HEAD].astype(F32), axis=-1, keepdims=True)
            lse = jnp.broadcast_to(lse, (SLAB, HEAD))
            lse_s[part] = lse
            top = jnp.maximum(top, lse)
        share = jnp.exp(fresh - top)
        total = share
        summed = share * vx[lines, :]
        for part in range(SEQS):
            share = jnp.exp(lse_s[part] - top)
            total = total + share
            summed = summed + share * orecv[part, :, 0:HEAD].astype(F32)
        ag[mine] = (summed / total).astype(BF16)
        to_seq(ag.at[mine], ag.at[mine], 3)
        drain(ag.at[pl.ds(0, OWNERS - 1)], recv_sem.at[3])

    @pl.when(jnp.logical_not(is_owner))
    def _():
        drain(ag, recv_sem.at[3])

    for index in range(OWNERS):
        af[SLAB * index : SLAB * (index + 1), :] = ag[index].astype(F32)
    for head in range(HEADS):
        normed[0:ROWS, HEAD * head : HEAD * (head + 1)] = af[pl.ds(head, ROWS, stride=HEADS), :].astype(BF16)
    loads[6].wait()
    mixed = xg[me].astype(F32) + matmul_nt(normed[0:ROWS, :], out_w[...])
    mg[me, me_req] = mixed.astype(BF16)

    to_req(mg.at[me, me_req], mg.at[me, me_req], 4)
    drain(mg.at[0, pl.ds(0, REQS - 1)], recv_sem.at[4])
    to_seq(mg.at[me], mg.at[me], 5)
    drain(mg.at[pl.ds(0, SEQS - 1)], recv_sem.at[5])
    for part in range(SEQS):
        for group in range(REQS):
            big[ROWS * group : ROWS * (group + 1), PART * part : PART * (part + 1)] = mg[part, group].astype(F32)
    loads[7].wait()
    normed[...] = normalized(big[...], gain2[...])
    loads[8].wait()
    gate = matmul_nt(normed[...], gate_w[...])
    loads[9].wait()
    up = matmul_nt(normed[...], up_w[...])
    hidden = (gate / (1.0 + jnp.exp(-gate)) * up).astype(BF16)
    loads[10].wait()
    for index in range(OWNERS):
        fs[index] = jnp.dot(
            hidden, down_w[:, COLUMNS * index : COLUMNS * (index + 1)], preferred_element_type=F32
        ).astype(BF16)

    to_owners(lambda index: fs.at[index], frecv.at[me], 6, load_sem.at[14])

    @pl.when(is_owner)
    def _():
        pltpu.make_async_copy(fs.at[mine], frecv.at[me], load_sem.at[14]).wait()
        drain(frecv.at[pl.ds(0, SEQS - 1)], recv_sem.at[6])
        partial = frecv[0].astype(F32)
        for part in range(1, SEQS):
            partial = partial + frecv[part].astype(F32)
        yex[me_req] = partial
        to_req(yex.at[me_req], yex.at[me_req], 7)
        drain(yex.at[pl.ds(0, REQS - 1)], recv_sem.at[7])
        feed = yex[0] + yex[1] + yex[2] + yex[3]
        columns = pl.ds(pl.multiple_of(mine * COLUMNS, COLUMNS), COLUMNS)
        rg[mine] = (big[:, columns] + feed).astype(BF16)
        to_seq(rg.at[mine], rg.at[mine], 8)
        drain(rg.at[pl.ds(0, OWNERS - 1)], recv_sem.at[8])

    @pl.when(jnp.logical_not(is_owner))
    def _():
        drain(rg, recv_sem.at[8])

    for index in range(OWNERS):
        big[:, COLUMNS * index : COLUMNS * (index + 1)] = rg[index].astype(F32)
    tile = (me * PART) // HEAD
    window = big[
        pl.ds(pl.multiple_of(me_req * ROWS, ROWS), ROWS), pl.ds(pl.multiple_of(tile * HEAD, HEAD), 2 * HEAD)
    ]
    block = window
    for quarter in range(1, 4):
        block = jnp.where(lax.rem(me, 4) == quarter, pltpu.roll(window, 256 - 32 * quarter, 1), block)
    states_ref[0] = block[:, 0:PART].astype(BF16)

    loads[11].wait()
    normed[...] = normalized(big[...], gain3[...])
    loads[12].wait()
    logits = jnp.dot(normed[...], head_w[...], preferred_element_type=F32)
    ids = (me_req * SEQS + me) * VOCAB_PART + lax.broadcasted_iota(jnp.int32, (ALL_ROWS, VOCAB_PART), 1)
    rows = lax.broadcasted_iota(jnp.int32, (ALL_ROWS, HEAD), 0)
    wanted = jnp.zeros((ALL_ROWS, HEAD), jnp.int32)
    for row in range(ALL_ROWS):
        wanted = jnp.where(rows == row, targets[0, row], wanted)
    picked = jnp.sum(jnp.where(ids == wanted[:, 0:1], logits, 0.0), axis=-1, keepdims=True)
    top = jnp.max(logits, axis=-1, keepdims=True)
    total = jnp.sum(jnp.exp(logits - top), axis=-1, keepdims=True)
    lanes = lax.broadcasted_iota(jnp.int32, (ALL_ROWS, HEAD), 1)
    stats = jnp.where(lanes == 0, top, jnp.where(lanes == 1, total, jnp.where(lanes == 2, picked, 0.0)))
    stats = jnp.concatenate([stats, jnp.zeros((HEAD - ALL_ROWS, HEAD), F32)], axis=0)
    st[me_req] = stats.T[0:8, :]

    to_req(st.at[me_req], st.at[me_req], 9)
    drain(st.at[pl.ds(0, REQS - 1)], recv_sem.at[9])

    def joined(ref):
        tops, totals, picks = ref[:, 0, :], ref[:, 1, :], ref[:, 2, :]
        highest = jnp.max(tops, axis=0, keepdims=True)
        whole = jnp.sum(totals * jnp.exp(tops - highest), axis=0, keepdims=True)
        return highest, whole, jnp.sum(picks, axis=0, keepdims=True)

    highest, whole, pick = joined(st)
    sub = lax.broadcasted_iota(jnp.int32, (8, HEAD), 0)
    sh[me] = jnp.where(sub == 0, highest, jnp.where(sub == 1, whole, pick))
    to_seq(sh.at[me], sh.at[me], 10)
    drain(sh.at[pl.ds(0, SEQS - 1)], recv_sem.at[10])
    highest, whole, pick = joined(sh)
    probs_ref[...] = (pick - (highest + jnp.log(whole)))[:, 0:ALL_ROWS]

    drain(xg.at[pl.ds(0, SEQS - 1)], send_sem.at[0])
    drain(pk.at[pl.ds(0, SEQS - 1)], send_sem.at[1])
    drain(mg.at[0, pl.ds(0, REQS - 1)], send_sem.at[4])
    drain(mg.at[pl.ds(0, SEQS - 1)], send_sem.at[5])
    drain(st.at[pl.ds(0, REQS - 1)], send_sem.at[9])
    drain(sh.at[pl.ds(0, SEQS - 1)], send_sem.at[10])

    @pl.when(is_owner)
    def _():
        drain(obuf.at[pl.ds(0, OWNERS - 1)], send_sem.at[2])
        drain(fs.at[pl.ds(0, OWNERS - 1)], send_sem.at[6])
        drain(yex.at[pl.ds(0, REQS - 1)], send_sem.at[7])
        drain(obuf_like(orecv, SEQS - 1), send_sem.at[3])
        drain(frecv.at[pl.ds(0, SEQS - 1)], send_sem.at[8])

    @pl.when(jnp.logical_not(is_owner))
    def _():
        drain(obuf, send_sem.at[2])
        drain(fs, send_sem.at[6])


def obuf_like(ref, count):
    return ref.at[pl.ds(0, count), :, pl.ds(0, HEAD)]


def per_device(
    inputs, lengths, targets, cache_keys, cache_values, attention_gain, packed_weight, packed_bias, out_weight,
    feedforward_gain, gate_weight, up_weight, down_weight, final_gain, head_weight,
):
    hbm = pl.BlockSpec(memory_space=pl.ANY)
    smem = pl.BlockSpec(memory_space=pltpu.SMEM)
    vmem = pl.BlockSpec(memory_space=pltpu.VMEM)

    def held(*shape, dtype=BF16):
        return pltpu.VMEM(shape, dtype)

    return pl.pallas_call(
        kernel,
        out_shape=(
            jax.ShapeDtypeStruct((1, ROWS, PART), BF16),
            jax.ShapeDtypeStruct((1, ALL_ROWS), F32),
        ),
        in_specs=[smem, smem] + [hbm] * 13,
        out_specs=(vmem, vmem),
        scratch_shapes=[
            held(ROWS, POSITIONS * KV, HEAD),
            held(ROWS, POSITIONS * KV, HEAD),
            held(1, WIDTH, dtype=F32),
            held(PACKED_PART, WIDTH),
            held(1, PACKED_PART, dtype=F32),
            held(PART, WIDTH),
            held(1, WIDTH, dtype=F32),
            held(FF_PART, WIDTH),
            held(FF_PART, WIDTH),
            held(FF_PART, WIDTH),
            held(1, WIDTH, dtype=F32),
            held(WIDTH, VOCAB_PART),
            held(SEQS, ROWS, PART),
            held(ALL_ROWS, WIDTH, dtype=F32),
            held(ALL_ROWS, WIDTH),
            held(SEQS, ROWS, PACKED_PART),
            held(ROWS, PACKED, dtype=F32),
            held(ROWS * HEADS, HEAD, dtype=F32),
            held(ROWS * HEADS, HEAD, dtype=F32),
            held(ROWS * HEADS, HEAD, dtype=F32),
            held(ROWS * HEADS, HEAD, dtype=F32),
            held(ROWS * HEADS, HEAD, dtype=F32),
            held(OWNERS, SLAB, 2 * HEAD),
            held(SEQS, SLAB, 2 * HEAD),
            held(SEQS, SLAB, HEAD, dtype=F32),
            held(OWNERS, SLAB, HEAD),
            held(ROWS * HEADS, HEAD, dtype=F32),
            held(SEQS, REQS, ROWS, PART),
            held(OWNERS, ALL_ROWS, COLUMNS),
            held(SEQS, ALL_ROWS, COLUMNS),
            held(REQS, ALL_ROWS, COLUMNS, dtype=F32),
            held(OWNERS, ALL_ROWS, COLUMNS),
            held(REQS, 8, HEAD, dtype=F32),
            held(SEQS, 8, HEAD, dtype=F32),
            pltpu.SemaphoreType.DMA((15,)),
            pltpu.SemaphoreType.DMA((11,)),
            pltpu.SemaphoreType.DMA((11,)),
        ],
        compiler_params=pltpu.CompilerParams(
            collective_id=0, has_side_effects=True, vmem_limit_bytes=60 * 1024 * 1024
        ),
        name="decode_step",
    )(
        lengths,
        targets,
        inputs,
        cache_keys.reshape(ROWS, POSITIONS * KV, HEAD),
        cache_values.reshape(ROWS, POSITIONS * KV, HEAD),
        attention_gain.reshape(1, WIDTH),
        packed_weight.T,
        packed_bias.reshape(1, PACKED_PART),
        out_weight.T,
        feedforward_gain.reshape(1, WIDTH),
        gate_weight.T,
        up_weight.T,
        down_weight,
        final_gain.reshape(1, WIDTH),
        head_weight,
    )


def solution(mesh):
    return jax.shard_map(
        per_device,
        mesh=mesh,
        in_specs=(
            P(None, "req", "seq"),
            P("req"),
            P(),
            P("req", "seq", None, None),
            P("req", "seq", None, None),
            P(),
            P(None, "seq"),
            P("seq"),
            P(None, "seq"),
            P(),
            P(None, ("req", "seq")),
            P(None, ("req", "seq")),
            P(("req", "seq"), None),
            P(),
            P(None, ("req", "seq")),
        ),
        out_specs=(P(None, "req", "seq"), P()),
        check_vma=False,
    )
```

time: 1060 us -> 87 us (0.08)
  waiting for transfers between devices: 640 us -> 0 us
  blocking collectives: 304 us -> 0 us
  Pallas kernels: 0 us -> 83.8 us
  local copies, waits for them, and re-layouts: 44.6 us -> 2.4 us
  other arithmetic: 38.1 us -> 0 us
  matrix products: 19.2 us -> 0 us
  between operations: 14.4 us -> 0.64 us
    reduce_scatter x1 -> x0, waiting for transfers between devices: 640 us -> none  [per_device(): lax.psum_scatter(arranged, ('req', 'seq'), scatter_dimension=0, tiled=True)]
    all_gather x8 -> x0, blocking collectives: 174 us -> none  [the longest x3 80.2 us: full_features(): return lax.all_gather(block, 'seq', axis=1, tiled=True)]
    pallas_call x0 -> x1, Pallas kernels: none -> 83.8 us  [per_device(): pl.pallas_call(kernel, out_shape=(jax.ShapeDtypeStruct((1, ROWS, PART), B...]
    pmax x1 -> x0, blocking collectives: 66 us -> none  [per_device(): global_top = lax.pmax(logits.max(axis=-1), ('req', 'seq'))]
    psum x1 -> x0, blocking collectives: 64.4 us -> none  [per_device(): lax.psum((jnp.sum(jnp.exp(logits - global_top[:, None]), axis=-1), picked...]
    add x65 -> x0, other arithmetic: 31.4 us -> none  [the longest x32 23.6 us: join_parts(): total = earlier[1] * factor_one + later[1] * factor_two]
    dynamic_slice x34 -> x0, local copies, waits for them, and re-layouts: 29.9 us -> none  [take(): lax.dynamic_index_in_dim(a, source, 0, False)]
    dot_general x8 -> x0, matrix products: 19.2 us -> none  [the longest x1 4.85 us: per_device(): jnp.dot(hidden, down_weight, preferred_element_type=jnp.float32)]
  transfers between devices with their start and end apart: 2 -> 0, of which waited for: 1 -> 0; matrix products, arithmetic and copies ran while one was open for 0% -> 0% of each run, Pallas kernels for 0% -> 0%
where the time goes in v1:
time: 87 us; the launch traced here: 86.8 us
  Pallas kernels  83.8 us (96%)
  local copies, waits for them, and re-layouts  2.4 us (3%)
    pallas_call x1, Pallas kernels, per_device(): pl.pallas_call(kernel, out_shape=(jax.ShapeDtypeStruct((1, ROWS, PART), B...  83.8 us
    unnamed x2, local copies, waits for them, and re-layouts  2.4 us

profile of v1, /device:TPU:1, one launch (start us, length us, event | category | flops | bytes accessed | tf_op | source)
XLA Modules:
  0.0 86.8 jit_solution(11945109697419389807)
XLA Ops:
  0.6 83.8 %decode_step.1 = (bf16[1,8,160]{2,1,0:T(8,128)(2,1)}, f32[1,32]{1,0:T(1,128)}) custom-call(s32[8]{0:T(128)} %lengths.1, s32[1,32]{1,0:T(1,128)} %targets.1, bf16[1,8,160]{2,1,0:T(8,128)(2,1)} %x_hbm.1, bf16[8,1024,128]{2,1,0:T(8,128)(2,1)} %bitcast.13, bf16[8,1024,128]{2,1,0:T(8,128)(2,1)} %bitcast.14, f32[1,5120]{1,0:T(1,128)} %bitcast.16, ...), custom_call_target="tpu_custom_call" | custom-call | tf_op jit(solution)/shard_map/decode_step/pallas_call | solution.py:382
  84.4 1.3 %copy.19 = bf16[1,8,160]{2,1,0:T(8,128)(2,1)} copy(bf16[1,8,160]{2,1,0:T(8,128)(2,1)} %get-tuple-element.4) | data formatting | bytes 5120
  85.7 1.1 %copy.20 = f32[1,32]{1,0:T(1,128)} copy(f32[1,32]{1,0:T(1,128)} %get-tuple-element.5) | data formatting | bytes 256
